TPU v7x, 32 devices: a whole 2x2x4 slice. The times are simulated.
32 devices in a mesh: gx: 4 (over z), gy: 4 (over x, core), gz: 2 (over y).
Axes of the slice: x: 2, y: 2, z: 4, core: 2. Of those that a mesh axis runs over, the one named last changes fastest.
Arguments:
- activations: bfloat16 [1024, 8192], P('gy', 'gx'), may hold values from -0.5 to 0.5
- cotangent: bfloat16 [1024, 8192], P('gy', 'gx'), may hold values from -1.5 to 1.5
- gate_pre: bfloat16 [1024, 26624], P('gx', ('gy', 'gz')), may hold values from -6 to 6
- up_pre: bfloat16 [1024, 26624], P('gx', ('gy', 'gz')), may hold values from -6 to 6
- gate_weight: bfloat16 [8192, 26624], P('gx', ('gy', 'gz')), may hold values from -0.0625 to 0.0625
- up_weight: bfloat16 [8192, 26624], P('gx', ('gy', 'gz')), may hold values from -0.0625 to 0.0625
- down_weight: bfloat16 [26624, 8192], P(('gy', 'gz'), 'gx'), may hold values from -0.15625 to 0.15625
Outputs:
- input_grad: bfloat16 [1024, 8192], P('gy', 'gx')
- gate_grad: bfloat16 [8192, 26624], P('gx', ('gy', 'gz'))
- up_grad: bfloat16 [8192, 26624], P('gx', ('gy', 'gz'))
- down_grad: bfloat16 [26624, 8192], P(('gy', 'gz'), 'gx')
All inputs are finite; a program needn't handle non-finite values.
Results may differ from a plain program's by a relative error of at most 0.015.
Values may be sent and summed in bfloat16 or wider, within the bound.
A program may use at most 192 MiB of HBM per device.

v0:
```python
import jax
import jax.numpy as jnp
from jax import lax
from jax.sharding import PartitionSpec as P

over_rows = (((0,), (0,)), ((), ()))
over_cols = (((1,), (1,)), ((), ()))


def swiglu_grads(gate_in, up_in, grad_hidden):
    gate_val = gate_in.astype(jnp.float32)
    up_val = up_in.astype(jnp.float32)
    sigmoid = jax.nn.sigmoid(gate_val)
    hidden = (gate_val * sigmoid * up_val).astype(jnp.bfloat16)
    grad_gate = (grad_hidden * up_val * sigmoid * (1.0 + gate_val * (1.0 - sigmoid))).astype(
        jnp.bfloat16
    )
    grad_up = (grad_hidden * gate_val * sigmoid).astype(jnp.bfloat16)
    return (hidden, grad_gate, grad_up)


def input_terms(grad_gate, grad_up, gate_weight, up_weight):

    def compute(offset, amount):
        total = lax.dot_general(
            grad_gate, gate_weight, over_cols, preferred_element_type=jnp.float32
        )
        return total + lax.dot_general(
            grad_up, up_weight, over_cols, preferred_element_type=jnp.float32
        )

    return compute


def shards(activations, cotangent, gate_pre, up_pre, gate_weight, up_weight, down_weight):
    cotangent_all = lax.all_gather(cotangent, "gy", axis=0, tiled=True)
    gate_all, up_all = (
        lax.all_gather(gate_pre, "gx", axis=0, tiled=True),
        lax.all_gather(up_pre, "gx", axis=0, tiled=True),
    )
    local_sum = lax.dot_general(
        cotangent_all, down_weight, over_cols, preferred_element_type=jnp.float32
    )
    grad_hidden = lax.psum(local_sum, "gx")
    hidden, grad_gate, grad_up = swiglu_grads(gate_all, up_all, grad_hidden)
    down_grad = lax.dot_general(
        hidden, cotangent_all, over_rows, preferred_element_type=jnp.float32
    ).astype(jnp.bfloat16)
    segment = lax.all_gather(activations, "gy", axis=0, tiled=True)
    first = lax.dot_general(segment, grad_gate, over_rows, preferred_element_type=jnp.float32)
    second = lax.dot_general(segment, grad_up, over_rows, preferred_element_type=jnp.float32)
    row_count = activations.shape[0]
    terms = input_terms(grad_gate, grad_up, gate_weight, up_weight)
    share_rows = row_count // lax.axis_size("gz")
    input_share = lax.psum_scatter(
        terms(jnp.int32(0), lax.axis_size(("gy", "gz")) * share_rows),
        ("gy", "gz"),
        scatter_dimension=0,
        tiled=True,
    )
    input_grad = lax.all_gather(input_share.astype(jnp.bfloat16), "gz", axis=0, tiled=True)
    return (input_grad, first.astype(jnp.bfloat16), second.astype(jnp.bfloat16), down_grad)


def solution(mesh):
    in_specs = (
        P("gy", "gx"),
        P("gy", "gx"),
        P("gx", ("gy", "gz")),
        P("gx", ("gy", "gz")),
        P("gx", ("gy", "gz")),
        P("gx", ("gy", "gz")),
        P(("gy", "gz"), "gx"),
    )
    out_specs = (P("gy", "gx"), P("gx", ("gy", "gz")), P("gx", ("gy", "gz")), P(("gy", "gz"), "gx"))
    return jax.shard_map(shards, mesh=mesh, in_specs=in_specs, out_specs=out_specs, check_vma=False)
```

profile of v0, /device:TPU:0, one launch (start us, length us, event | category | flops | bytes accessed | tf_op | source)
XLA Modules:
  0.0 951.3 jit_solution(15693381875679629747)
XLA Ops:
  7.2 0.0 all-gather.6.cloned.1.call-start
  7.2 0.7 all-gather.6.cloned.1.call-update
  7.9 0.0 all-gather.10.cloned.1.call-start
  7.9 0.7 all-gather.10.cloned.1.call-update
  8.6 0.0 all-gather.8.cloned.1.call-start
  8.7 0.7 all-gather.8.cloned.1.call-update
  9.4 0.0 all-reduce.2.cloned.1.call-start
  9.4 37.3 %all-gather.6.cloned.1.call-done = bf16[1024,2048]{1,0:T(8,128)(2,1)} async-done(((bf16[256,2048]{1,0:T(8,128)(2,1)}), bf16[1024,2048]{1,0:T(8,128)(2,1)}) %all-gather.6.cloned.1.call-update) | async-done | bytes 4194320 | tf_op jit(solution)/shard_map/all_gather | solution.py:36
  46.8 22.5 %fusion.17 = f32[1024,3328]{1,0:T(8,128)} fusion(bf16[1024,2048]{1,0:T(8,128)(2,1)} %all-gather.6.cloned.1.call-done, bf16[3328,2048]{1,0:T(8,128)(2,1)} %param.13), kind=kOutput, calls=%fused_computation.24 | convolution fusion | flops 13958643712 | bytes 31457280 | tf_op jit(solution)/shard_map/dot_general | solution.py:41
  69.3 0.0 all-reduce.2.cloned.1.call-update
  69.3 0.0 all-gather.14.cloned.1.call-start
  69.4 0.5 all-gather.14.cloned.1.call-update
  69.9 0.2 reduce-scatter.2.cloned.1.call-start
  70.2 102.1 %all-gather.10.cloned.1.call-done = bf16[1024,3328]{1,0:T(8,128)(2,1)} async-done(((bf16[256,3328]{1,0:T(8,128)(2,1)}), bf16[1024,3328]{1,0:T(8,128)(2,1)}) %all-gather.10.cloned.1.call-update) | async-done | bytes 6815760 | tf_op jit(solution)/shard_map/all_gather | solution.py:38
  172.3 123.8 %all-gather.8.cloned.1.call-done = bf16[1024,3328]{1,0:T(8,128)(2,1)} async-done(((bf16[256,3328]{1,0:T(8,128)(2,1)}), bf16[1024,3328]{1,0:T(8,128)(2,1)}) %all-gather.8.cloned.1.call-update) | async-done | bytes 6815760 | tf_op jit(solution)/shard_map/all_gather | solution.py:39
  296.1 461.1 %all-reduce.2.cloned.1.call-done = f32[1024,3328]{1,0:T(8,128)} async-done(((f32[1024,3328]{1,0:T(8,128)}), f32[1024,3328]{1,0:T(8,128)}) %all-reduce.2.cloned.1.call-update) | async-done | bytes 13631504 | tf_op jit(solution)/shard_map/psum | solution.py:44
  757.1 12.2 %fusion.2 = bf16[1024,3328]{1,0:T(8,128)(2,1)S(1)} fusion(f32[1024,3328]{1,0:T(8,128)} %all-reduce.2.cloned.1.call-done, bf16[1024,3328]{1,0:T(8,128)(2,1)} %all-gather.8.cloned.1.call-done, bf16[1024,3328]{1,0:T(8,128)(2,1)} %all-gather.10.cloned.1.call-done), kind=kLoop, calls=%fused_computation.11 | loop fusion | flops 40894464 | bytes 34078720 | tf_op jit(solution)/shard_map/convert_element_type | solution.py:15
  769.3 0.0 copy-start
  769.3 2.9 copy-done
  772.2 18.1 %fusion.18 = f32[1024,2048]{1,0:T(8,128)} fusion(bf16[1024,3328]{1,0:T(8,128)(2,1)S(1)} %fusion.2, bf16[2048,3328]{1,0:T(8,128)(2,1)} %param.11), kind=kOutput, calls=%fused_computation.25 | convolution fusion | flops 13958643712 | bytes 28835840 | tf_op jit(solution)/shard_map/dot_general | solution.py:25
  790.3 24.1 %convolution_add_fusion = f32[1024,2048]{1,0:T(8,128)} fusion(f32[1024,2048]{1,0:T(8,128)} %fusion.18, bf16[2048,3328]{1,0:T(8,128)(2,1)} %param.12, f32[1024,3328]{1,0:T(8,128)} %all-reduce.2.cloned.1.call-done, bf16[1024,3328]{1,0:T(8,128)(2,1)} %all-gather.10.cloned.1.call-done), kind=kOutput, calls=%fused_computation.22 | convolution fusion | flops 13984595968 | bytes 50855936 | tf_op jit(solution)/shard_map/dot_general | solution.py:28
  814.4 0.0 reduce-scatter.2.cloned.1.call-update
  814.4 0.3 all-gather.12.cloned.1.call-start
  814.7 23.9 %convolution_convert_fusion = bf16[3328,2048]{1,0:T(8,128)(2,1)} fusion(bf16[1024,2048]{1,0:T(8,128)(2,1)} %all-gather.6.cloned.1.call-done, bf16[1024,3328]{1,0:T(8,128)(2,1)} %all-gather.8.cloned.1.call-done, bf16[1024,3328]{1,0:T(8,128)(2,1)} %all-gather.10.cloned.1.call-done), kind=kOutput, calls=%fused_computation.6 | convolution fusion | flops 13992722432 | bytes 31457280 | tf_op jit(solution)/shard_map/dot_general | solution.py:46
  838.6 0.0 all-gather.14.cloned.1.call-done
  838.6 23.5 %fusion.11 = bf16[2048,3328]{0,1:T(8,128)(2,1)} fusion(bf16[1024,2048]{1,0:T(8,128)(2,1)} %all-gather.14.cloned.1.call-done, f32[1024,3328]{1,0:T(8,128)} %all-reduce.2.cloned.1.call-done, bf16[1024,3328]{1,0:T(8,128)(2,1)} %all-gather.10.cloned.1.call-done), kind=kOutput, calls=%fused_computation.20 | convolution fusion | flops 13989314560 | bytes 38273024 | tf_op jit(solution)/shard_map/dot_general | solution.py:51
  862.1 22.0 %reduce-scatter.2.cloned.1.call-done = f32[128,2048]{1,0:T(8,128)} async-done(((f32[1024,2048]{1,0:T(8,128)}), f32[128,2048]{1,0:T(8,128)}) %reduce-scatter.2.cloned.1.call-update) | async-done | bytes 1048592 | tf_op jit(solution)/shard_map/reduce_scatter | solution.py:55
  884.1 2.1 convert_element_type.37
  886.2 0.0 all-gather.12.cloned.1.call-update
  886.2 21.0 %fusion.10 = bf16[2048,3328]{0,1:T(8,128)(2,1)} fusion(bf16[1024,3328]{1,0:T(8,128)(2,1)} %copy-done, bf16[1024,2048]{1,0:T(8,128)(2,1)} %all-gather.14.cloned.1.call-done), kind=kOutput, calls=%fused_computation.19 | convolution fusion | flops 13965459456 | bytes 24641536 | tf_op jit(solution)/shard_map/dot_general | solution.py:50
  907.3 17.4 %copy.11 = bf16[2048,3328]{1,0:T(8,128)(2,1)} copy(bf16[2048,3328]{0,1:T(8,128)(2,1)} %fusion.10) | data formatting | bytes 27262976
  924.7 17.4 %copy.12 = bf16[2048,3328]{1,0:T(8,128)(2,1)} copy(bf16[2048,3328]{0,1:T(8,128)(2,1)} %fusion.11) | data formatting | bytes 27262976
  942.1 0.0 all-gather.12.cloned.1.call-done
  942.2 2.3 copy.15
Async XLA Ops:
  7.2 39.6 %all-gather.6.cloned.1.call-start = ((), (), s32[]{:S(2)}) async-start(), calls=%async_computation.1 | async-start | bytes 5242880 | tf_op jit(solution)/shard_map/all_gather | solution.py:36
  7.9 164.4 %all-gather.10.cloned.1.call-start = ((), (), s32[]{:S(2)}) async-start(), calls=%async_computation.4 | async-start | bytes 8519680 | tf_op jit(solution)/shard_map/all_gather | solution.py:38
  8.6 287.4 %all-gather.8.cloned.1.call-start = ((), (), s32[]{:S(2)}) async-start(), calls=%async_computation.3 | async-start | bytes 8519680 | tf_op jit(solution)/shard_map/all_gather | solution.py:39
  9.4 747.8 %all-reduce.2.cloned.1.call-start = ((), (), s32[]{:S(2)}) async-start(), calls=%async_computation.2 | async-start | bytes 27262976 | tf_op jit(solution)/shard_map/psum | solution.py:44
  69.3 769.3 %all-gather.14.cloned.1.call-start = ((), (), s32[]{:S(2)}) async-start(), calls=%async_computation.7 | async-start | bytes 5242880 | tf_op jit(solution)/shard_map/all_gather | solution.py:49
  69.9 814.2 %reduce-scatter.2.cloned.1.call-start = ((), (), s32[]{:S(2)}) async-start(), calls=%async_computation.5 | async-start | bytes 9437184 | tf_op jit(solution)/shard_map/reduce_scatter | solution.py:55
  769.3 2.9 copy-start
  814.4 127.7 %all-gather.12.cloned.1.call-start = ((), (), s32[]{:S(2)}) async-start(), calls=%async_computation.6 | async-start | bytes 1572864 | tf_op jit(solution)/shard_map/all_gather | solution.py:61
Sparse Core Ops, SparseCore 0:
  9.6 37.1 all-gather.5
  48.3 123.9 all-gather.9
  173.9 122.1 all-gather.7
  299.0 458.1 all-reduce.1
  758.6 33.3 all-gather.13
  814.6 69.5 reduce-scatter.1
  886.4 21.2 all-gather.11
where the time goes:
time: 952 us; the launch traced here: 951 us
  waiting for transfers between devices  749 us (79%)
  matrix products  133 us (14%)
  local copies, waits for them, and re-layouts  40.1 us (4%)
  other arithmetic  14.3 us (2%)
  between operations  14.1 us (1%)
    psum x1, waiting for transfers between devices, shards(): grad_hidden = lax.psum(local_sum, 'gx')  461 us
    all_gather x1, waiting for transfers between devices, shards(): lax.all_gather(up_pre, 'gx', axis=0, tiled=True)  124 us
    all_gather x1, waiting for transfers between devices, shards(): lax.all_gather(gate_pre, 'gx', axis=0, tiled=True)  102 us
    unnamed x5, local copies, waits for them, and re-layouts  40.1 us
    all_gather x1, waiting for transfers between devices, shards(): cotangent_all = lax.all_gather(cotangent, 'gy', axis=0, tiled=True)  37.3 us
    dot_general x1, matrix products, compute(): lax.dot_general(grad_up, up_weight, over_cols, preferred_element_type=jnp...  24.1 us
    dot_general x1, matrix products, shards(): lax.dot_general(hidden, cotangent_all, over_rows, preferred_element_type=...  23.9 us
    dot_general x1, matrix products, shards(): lax.dot_general(segment, grad_up, over_rows, preferred_element_type=jnp.f...  23.5 us
  transfers between devices with their start and end apart: 7, of which 5 were waited for; matrix products, arithmetic and copies ran while one was open for 19% of the time, Pallas kernels for 0%

commit v1 on v0

--- a/solution.py
+++ b/solution.py
@@ -41,7 +41,7 @@
     local_sum = lax.dot_general(
         cotangent_all, down_weight, over_cols, preferred_element_type=jnp.float32
     )
-    grad_hidden = lax.psum(local_sum, "gx")
+    grad_hidden = jnp.sum(lax.all_gather(local_sum, "gx"), axis=0)
     hidden, grad_gate, grad_up = swiglu_grads(gate_all, up_all, grad_hidden)
     down_grad = lax.dot_general(
         hidden, cotangent_all, over_rows, preferred_element_type=jnp.float32

time: 952 us -> 1420 us (1.49)
  waiting for transfers between devices: 749 us -> 1190 us
  other arithmetic: 14.3 us -> 39.5 us
    all_gather x0 -> x1, waiting for transfers between devices: none -> 904 us  [shards(): grad_hidden = jnp.sum(lax.all_gather(local_sum, 'gx'), axis=0)]
    psum x1 -> x0, waiting for transfers between devices: 461 us -> none  [shards(): grad_hidden = lax.psum(local_sum, 'gx')]
    reduce_sum x0 -> x1, other arithmetic: none -> 25.1 us  [shards(): grad_hidden = jnp.sum(lax.all_gather(local_sum, 'gx'), axis=0)]
  transfers between devices with their start and end apart: 7 -> 7, of which waited for: 5 -> 5; matrix products, arithmetic and copies ran while one was open for 19% -> 13% of each run, Pallas kernels for 0% -> 0%
where the time goes in v1:
time: 1420 us
  waiting for transfers between devices  1190 us (84%)
  matrix products  133 us (9%)
  local copies, waits for them, and re-layouts  39.9 us (3%)
  other arithmetic  39.5 us (3%)
  between operations  14.4 us (1%)
    all_gather x1, waiting for transfers between devices, shards(): grad_hidden = jnp.sum(lax.all_gather(local_sum, 'gx'), axis=0)  904 us
    all_gather x1, waiting for transfers between devices, shards(): lax.all_gather(up_pre, 'gx', axis=0, tiled=True)  124 us
    all_gather x1, waiting for transfers between devices, shards(): lax.all_gather(gate_pre, 'gx', axis=0, tiled=True)  99 us
    unnamed x5, local copies, waits for them, and re-layouts  39.9 us
    all_gather x1, waiting for transfers between devices, shards(): cotangent_all = lax.all_gather(cotangent, 'gy', axis=0, tiled=True)  38.8 us
  transfers between devices with their start and end apart: 7, of which 5 were waited for; matrix products, arithmetic and copies ran while one was open for 13% of the time, Pallas kernels for 0%

profile of v1, /device:TPU:0, one launch (start us, length us, event | category | flops | bytes accessed | tf_op | source)
XLA Modules:
  0.0 1417.4 jit_solution(8570504821461788977)
XLA Ops:
  7.2 0.0 all-gather.8.cloned.1.call-start
  7.2 0.7 all-gather.8.cloned.1.call-update
  7.9 0.0 all-gather.18.cloned.1.call-start
  7.9 38.8 %all-gather.8.cloned.1.call-done = bf16[1024,2048]{1,0:T(8,128)(2,1)} async-done(((bf16[256,2048]{1,0:T(8,128)(2,1)}), bf16[1024,2048]{1,0:T(8,128)(2,1)}) %all-gather.8.cloned.1.call-update) | async-done | bytes 4194320 | tf_op jit(solution)/shard_map/all_gather | solution.py:36
  46.8 22.5 %fusion.17 = f32[1024,3328]{1,0:T(8,128)} fusion(bf16[1024,2048]{1,0:T(8,128)(2,1)} %all-gather.8.cloned.1.call-done, bf16[3328,2048]{1,0:T(8,128)(2,1)} %param.13), kind=kOutput, calls=%fused_computation.24 | convolution fusion | flops 13958643712 | bytes 31457280 | tf_op jit(solution)/shard_map/dot_general | solution.py:41
  69.3 0.0 all-gather.18.cloned.1.call-update
  69.3 0.0 all-gather.12.cloned.1.call-start
  69.4 0.7 all-gather.12.cloned.1.call-update
  70.1 0.0 all-gather.10.cloned.1.call-start
  70.1 0.5 all-gather.10.cloned.1.call-update
  70.7 0.0 all-gather.16.cloned.1.call-start
  70.7 0.5 all-gather.16.cloned.1.call-update
  71.2 0.3 reduce-scatter.2.cloned.1.call-start
  71.6 904.0 %all-gather.18.cloned.1.call-done = f32[4096,3328]{1,0:T(8,128)} async-done(((f32[1024,3328]{1,0:T(8,128)}), f32[4096,3328]{1,0:T(8,128)}) %all-gather.18.cloned.1.call-update) | async-done | bytes 54525968 | tf_op jit(solution)/shard_map/all_gather | solution.py:44
  975.6 25.1 %reduce_sum.9 = f32[1024,3328]{1,0:T(8,128)} reduce(f32[4,1024,3328]{2,1,0:T(8,128)} %bitcast.14, f32[]{:T(128)} %constant.0.clone.1), dimensions={0}, to_apply=%region_0.0 | reduce | flops 10223616 | bytes 68157440 | tf_op jit(solution)/shard_map/reduce_sum | solution.py:44
  1000.7 99.0 %all-gather.12.cloned.1.call-done = bf16[1024,3328]{1,0:T(8,128)(2,1)} async-done(((bf16[256,3328]{1,0:T(8,128)(2,1)}), bf16[1024,3328]{1,0:T(8,128)(2,1)}) %all-gather.12.cloned.1.call-update) | async-done | bytes 6815760 | tf_op jit(solution)/shard_map/all_gather | solution.py:38
  1099.7 123.6 %all-gather.10.cloned.1.call-done = bf16[1024,3328]{1,0:T(8,128)(2,1)} async-done(((bf16[256,3328]{1,0:T(8,128)(2,1)}), bf16[1024,3328]{1,0:T(8,128)(2,1)}) %all-gather.10.cloned.1.call-update) | async-done | bytes 6815760 | tf_op jit(solution)/shard_map/all_gather | solution.py:39
  1223.3 12.3 fusion.2
  1235.6 0.0 copy-start
  1235.6 2.7 copy-done
  1238.3 18.1 %fusion.18 = f32[1024,2048]{1,0:T(8,128)} fusion(bf16[1024,3328]{1,0:T(8,128)(2,1)S(1)} %fusion.2, bf16[2048,3328]{1,0:T(8,128)(2,1)} %param.11), kind=kOutput, calls=%fused_computation.25 | convolution fusion | flops 13958643712 | bytes 28835840 | tf_op jit(solution)/shard_map/dot_general | solution.py:25
  1256.5 24.0 %convolution_add_fusion = f32[1024,2048]{1,0:T(8,128)} fusion(f32[1024,2048]{1,0:T(8,128)} %fusion.18, bf16[2048,3328]{1,0:T(8,128)(2,1)} %param.12, f32[1024,3328]{1,0:T(8,128)} %reduce_sum.9, bf16[1024,3328]{1,0:T(8,128)(2,1)} %all-gather.12.cloned.1.call-done), kind=kOutput, calls=%fused_computation.22 | convolution fusion | flops 13984595968 | bytes 50855936 | tf_op jit(solution)/shard_map/dot_general | solution.py:28
  1280.5 0.0 reduce-scatter.2.cloned.1.call-update
  1280.5 0.6 all-gather.14.cloned.1.call-start
  1281.1 24.0 %convolution_convert_fusion = bf16[3328,2048]{1,0:T(8,128)(2,1)} fusion(bf16[1024,2048]{1,0:T(8,128)(2,1)} %all-gather.8.cloned.1.call-done, bf16[1024,3328]{1,0:T(8,128)(2,1)} %all-gather.10.cloned.1.call-done, bf16[1024,3328]{1,0:T(8,128)(2,1)} %all-gather.12.cloned.1.call-done), kind=kOutput, calls=%fused_computation.6 | convolution fusion | flops 13992722432 | bytes 31457280 | tf_op jit(solution)/shard_map/dot_general | solution.py:46
  1305.0 0.0 all-gather.16.cloned.1.call-done
  1305.0 23.7 %fusion.11 = bf16[2048,3328]{0,1:T(8,128)(2,1)} fusion(bf16[1024,2048]{1,0:T(8,128)(2,1)} %all-gather.16.cloned.1.call-done, f32[1024,3328]{1,0:T(8,128)} %reduce_sum.9, bf16[1024,3328]{1,0:T(8,128)(2,1)} %all-gather.12.cloned.1.call-done), kind=kOutput, calls=%fused_computation.20 | convolution fusion | flops 13989314560 | bytes 38273024 | tf_op jit(solution)/shard_map/dot_general | solution.py:51
  1328.8 21.4 %reduce-scatter.2.cloned.1.call-done = f32[128,2048]{1,0:T(8,128)} async-done(((f32[1024,2048]{1,0:T(8,128)}), f32[128,2048]{1,0:T(8,128)}) %reduce-scatter.2.cloned.1.call-update) | async-done | bytes 1048592 | tf_op jit(solution)/shard_map/reduce_scatter | solution.py:55
  1350.1 2.1 convert_element_type.37
  1352.2 0.0 all-gather.14.cloned.1.call-update
  1352.2 20.9 %fusion.10 = bf16[2048,3328]{0,1:T(8,128)(2,1)} fusion(bf16[1024,3328]{1,0:T(8,128)(2,1)} %copy-done, bf16[1024,2048]{1,0:T(8,128)(2,1)} %all-gather.16.cloned.1.call-done), kind=kOutput, calls=%fused_computation.19 | convolution fusion | flops 13965459456 | bytes 24641536 | tf_op jit(solution)/shard_map/dot_general | solution.py:50
  1373.2 17.4 %copy.11 = bf16[2048,3328]{1,0:T(8,128)(2,1)} copy(bf16[2048,3328]{0,1:T(8,128)(2,1)} %fusion.10) | data formatting | bytes 27262976
  1390.6 17.4 %copy.12 = bf16[2048,3328]{1,0:T(8,128)(2,1)} copy(bf16[2048,3328]{0,1:T(8,128)(2,1)} %fusion.11) | data formatting | bytes 27262976
  1408.1 0.0 all-gather.14.cloned.1.call-done
  1408.1 2.3 copy.14
Async XLA Ops:
  7.2 39.6 %all-gather.8.cloned.1.call-start = ((), (), s32[]{:S(2)}) async-start(), calls=%async_computation.1 | async-start | bytes 5242880 | tf_op jit(solution)/shard_map/all_gather | solution.py:36
  7.9 967.7 %all-gather.18.cloned.1.call-start = ((), (), s32[]{:S(2)}) async-start(), calls=%async_computation.7 | async-start | bytes 68157440 | tf_op jit(solution)/shard_map/all_gather | solution.py:44
  69.3 1030.3 %all-gather.12.cloned.1.call-start = ((), (), s32[]{:S(2)}) async-start(), calls=%async_computation.3 | async-start | bytes 8519680 | tf_op jit(solution)/shard_map/all_gather | solution.py:38
  70.1 1153.2 %all-gather.10.cloned.1.call-start = ((), (), s32[]{:S(2)}) async-start(), calls=%async_computation.2 | async-start | bytes 8519680 | tf_op jit(solution)/shard_map/all_gather | solution.py:39
  70.7 1234.4 %all-gather.16.cloned.1.call-start = ((), (), s32[]{:S(2)}) async-start(), calls=%async_computation.6 | async-start | bytes 5242880 | tf_op jit(solution)/shard_map/all_gather | solution.py:49
  71.2 1278.9 %reduce-scatter.2.cloned.1.call-start = ((), (), s32[]{:S(2)}) async-start(), calls=%async_computation.4 | async-start | bytes 9437184 | tf_op jit(solution)/shard_map/reduce_scatter | solution.py:55
  1235.6 2.7 copy-start
  1280.5 127.5 %all-gather.14.cloned.1.call-start = ((), (), s32[]{:S(2)}) async-start(), calls=%async_computation.5 | async-start | bytes 1572864 | tf_op jit(solution)/shard_map/all_gather | solution.py:61
Sparse Core Ops, SparseCore 0:
  9.6 37.1 all-gather.7
  69.5 906.0 all-gather.17
  977.2 122.4 all-gather.11
  1101.1 122.1 all-gather.9
  1224.7 32.6 all-gather.15
  1280.6 69.4 reduce-scatter.1
  1352.4 21.2 all-gather.13
